TPU v7x, 256 devices: a whole 4x4x8 slice. The times are simulated.
256 devices in a mesh: ex: 8 (over z), ey: 4 (over x_hi, core), ez: 8 (over y, x_lo).
Axes of the slice: x: 4 (x_hi: 2, x_lo: 2; x = x_hi * 2 + x_lo), y: 4, z: 8, core: 2. Of those that a mesh axis runs over, the one named last changes fastest.
Arguments:
- load_raw: float32 [16, 8, 32, 32, 384], P('ex', 'ey', 'ez'), may hold values from -8 to 8
- scaling: float32 [16, 8, 32, 384], P('ex', 'ey', 'ez'), may hold values from 0.6 to 1.8
- fine_matrix: float32 [384, 384], replicated
- fine_inverse: float32 [384, 384], replicated
- prolong_four: float32 [384, 98], replicated
- coarse_four: float32 [98, 98], replicated
- prolong_two: float32 [384, 26], replicated
- coarse_two: float32 [26, 26], replicated
- orient: int32 [3, 16, 8, 32], P(None, 'ex', 'ey', 'ez'), may hold values from 0 to 3
- boundary: int32 [6, 16, 8, 32], P(None, 'ex', 'ey', 'ez'), may hold values from 0 to 1
Outputs:
- solution: float32 [16, 8, 32, 32, 384], P('ex', 'ey', 'ez')
All inputs are finite; a program needn't handle non-finite values.
Results may differ from a plain program's by a relative error of at most 0.0001.
Values sent between devices are 32-bit elements; how exact they have to be, the bound alone decides.
A program may use at most 64 MiB of HBM per device.

v0:
```python
import jax
import jax.numpy as jnp
from jax import lax
from jax.sharding import PartitionSpec as P

FACE_SIDE = 8
CYCLES = 2


fine_weight = 0.5
coarse_weight = 0.5


def passed_along(value, axis, steps):
    count = lax.axis_size(axis)
    leading, last = (max(0, -steps), min(count, count - steps))
    return lax.ppermute(value, axis, [(source, source + steps) for source in range(leading, last)])


def flip_face(face_data, face_code):
    reshaped = face_data.reshape(face_data.shape[:-1] + (FACE_SIDE, FACE_SIDE))
    codes_full = face_code[:, :, :, None, None, None]
    reshaped = jnp.where(codes_full % 2 == 1, jnp.flip(reshaped, -2), reshaped)
    reshaped = jnp.where(codes_full // 2 == 1, jnp.flip(reshaped, -1), reshaped)
    return reshaped.reshape(face_data.shape)


def keep_factors(boundary, dim_index, offset, total):
    position = lax.broadcasted_iota(jnp.int32, boundary.shape[1:], dim_index) + offset
    keep_low = 1 - jnp.where(position == 0, boundary[2 * dim_index], 0)
    keep_top = 1 - jnp.where(position == total - 1, boundary[2 * dim_index + 1], 0)
    return (keep_low.astype(jnp.float32), keep_top.astype(jnp.float32))


def one_axis(
    low_face, top_face, sent_low, face_code, dim_index, from_upper, from_lower, keep_low, keep_top
):
    count_along = low_face.shape[dim_index]
    above = jnp.concatenate(
        [lax.slice_in_dim(sent_low, 1, count_along, axis=dim_index), from_upper], dim_index
    )
    below = flip_face(
        jnp.concatenate(
            [from_lower, lax.slice_in_dim(top_face, 0, count_along - 1, axis=dim_index)], dim_index
        ),
        face_code,
    )
    return (
        (low_face + below) * keep_low[:, :, :, None, None],
        (top_face + above) * keep_top[:, :, :, None, None],
    )


def assemble(element_data, orient, boundary):
    face_nodes = element_data.shape[-1] // 6
    face_list = [
        element_data[..., face_index * face_nodes : (face_index + 1) * face_nodes]
        for face_index in range(6)
    ]
    count_x = element_data.shape[0]
    count_y = element_data.shape[1]
    count_z = element_data.shape[2]
    sent_x = flip_face(face_list[0], orient[0])
    sent_y = flip_face(face_list[2], orient[1])
    sent_z = flip_face(face_list[4], orient[2])
    upper_x = passed_along(sent_x[0:1], "ex", -1)
    lower_x = passed_along(face_list[1][count_x - 1 :], "ex", 1)
    upper_y = passed_along(sent_y[:, 0:1], "ey", -1)
    lower_y = passed_along(face_list[3][:, count_y - 1 :], "ey", 1)
    upper_z = passed_along(sent_z[:, :, 0:1], "ez", -1)
    lower_z = passed_along(face_list[5][:, :, count_z - 1 :], "ez", 1)
    keep_low_x, keep_top_x = keep_factors(
        boundary, 0, lax.axis_index("ex") * count_x, count_x * lax.axis_size("ex")
    )
    keep_low_y, keep_top_y = keep_factors(
        boundary, 1, lax.axis_index("ey") * count_y, count_y * lax.axis_size("ey")
    )
    keep_low_z, keep_top_z = keep_factors(
        boundary, 2, lax.axis_index("ez") * count_z, count_z * lax.axis_size("ez")
    )
    low_x, top_x = one_axis(
        face_list[0], face_list[1], sent_x, orient[0], 0, upper_x, lower_x, keep_low_x, keep_top_x
    )
    low_y, top_y = one_axis(
        face_list[2], face_list[3], sent_y, orient[1], 1, upper_y, lower_y, keep_low_y, keep_top_y
    )
    low_z, top_z = one_axis(
        face_list[4], face_list[5], sent_z, orient[2], 2, upper_z, lower_z, keep_low_z, keep_top_z
    )
    return jnp.concatenate([low_x, top_x, low_y, top_y, low_z, top_z], -1)


def product(left, right):
    return jnp.dot(left, right, precision=lax.Precision.HIGHEST, preferred_element_type=jnp.float32)


def apply_operator(solution, scaling, fine_matrix):
    nodes_count = solution.shape[-1]
    scaled = solution * scaling[:, :, :, None, :]
    row_block = product(scaled.reshape(-1, nodes_count), fine_matrix).reshape(solution.shape)
    return row_block * scaling[:, :, :, None, :]


def smooth_levels(
    residual, scaling, fine_inverse, prolong_four, coarse_four, prolong_two, coarse_two
):
    nodes_count = residual.shape[-1]
    inverse_scale = 1.0 / scaling[:, :, :, None, :]
    scaled = (residual * inverse_scale).reshape(-1, nodes_count)
    fine_term = fine_weight * product(scaled, fine_inverse)
    four_term = coarse_weight * product(
        product(product(scaled, prolong_four), coarse_four), prolong_four.T
    )
    two_term = coarse_weight * product(
        product(product(scaled, prolong_two), coarse_two), prolong_two.T
    )
    return (fine_term + four_term + two_term).reshape(residual.shape) * inverse_scale


def body(
    load_raw,
    scaling,
    fine_matrix,
    fine_inverse,
    prolong_four,
    coarse_four,
    prolong_two,
    coarse_two,
    orient,
    boundary,
):
    assembled = assemble(load_raw, orient, boundary)
    solution = jnp.zeros_like(load_raw)
    for cycle_index in range(CYCLES):
        if cycle_index == 0:
            residual = assembled
        else:
            residual = assembled - assemble(
                apply_operator(solution, scaling, fine_matrix), orient, boundary
            )
        smoothed = smooth_levels(
            residual, scaling, fine_inverse, prolong_four, coarse_four, prolong_two, coarse_two
        )
        solution = solution + assemble(smoothed, orient, boundary)
    return solution


def solution(mesh):
    in_specs = (
        P("ex", "ey", "ez", None, None),
        P("ex", "ey", "ez", None),
        P(),
        P(),
        P(),
        P(),
        P(),
        P(),
        P(None, "ex", "ey", "ez"),
        P(None, "ex", "ey", "ez"),
    )
    out_specs = P("ex", "ey", "ez", None, None)
    return jax.shard_map(body, mesh=mesh, in_specs=in_specs, out_specs=out_specs, check_vma=False)
```

profile of v0, /device:TPU:1, one launch (start us, length us, event | category | flops | bytes accessed | tf_op | source)
XLA Modules:
  0.0 277.8 jit_solution(17419910776081624638)
XLA Ops:
  2.1 5.1 %collective-permute-start = (f32[1,2,4,32,64]{3,4,2,1,0:T(8,128)}, f32[1,2,4,32,64]{3,4,2,1,0:T(8,128)}, u32[]{:S(2)}, u32[]{:S(2)}) collective-permute-start(f32[1,2,4,32,64]{3,4,2,1,0:T(8,128)} %copy.75), channel_id=1, source_target_pairs={{0,32},{32,64},{64,96},{96,128},{128,160},{160,192},{192,224},{1,3... | collective-permute-start | bytes 196616 | tf_op jit(solution)/shard_map/ppermute | solution.py:17
  8.0 3.7 %collective-permute-start.4 = (f32[2,2,1,32,64]{3,4,2,1,0:T(8,128)}, f32[2,2,1,32,64]{3,4,2,1,0:T(8,128)}, u32[]{:S(2)}, u32[]{:S(2)}) collective-permute-start(f32[2,2,1,32,64]{3,4,2,1,0:T(8,128)} %copy.81), channel_id=1, source_target_pairs={{0,1},{1,2},{2,3},{3,4},{4,5},{5,6},{6,7},{8,9},{9,10},{10,11},{11... | collective-permute-start | bytes 98312 | tf_op jit(solution)/shard_map/ppermute | solution.py:17
  12.7 5.5 %collective-permute-start.2 = (f32[2,1,4,32,64]{3,4,2,1,0:T(8,128)}, f32[2,1,4,32,64]{3,4,2,1,0:T(8,128)}, u32[]{:S(2)}, u32[]{:S(2)}) collective-permute-start(f32[2,1,4,32,64]{3,4,2,1,0:T(8,128)} %copy.77), channel_id=1, source_target_pairs={{0,8},{8,16},{16,24},{1,9},{9,17},{17,25},{2,10},{10,18},{18,26},{... | collective-permute-start | bytes 196616 | tf_op jit(solution)/shard_map/ppermute | solution.py:17
  47.5 5.6 %collective-permute-done.3 = f32[2,1,4,32,64]{4,3,2,1,0:T(8,128)S(1)} collective-permute-done((f32[2,1,4,32,64]{4,3,2,1,0:T(8,128)S(1)}, f32[2,1,4,32,64]{4,3,2,1,0:T(8,128)S(1)}, u32[]{:S(2)}, u32[]{:S(2)}) %collective-permute-start.3) | collective-permute-done | bytes 65568 | tf_op jit(solution)/shard_map/ppermute | solution.py:17
  59.9 4.0 %collective-permute-start.10 = (f32[2,2,1,32,64]{4,3,2,1,0:T(8,128)S(1)}, f32[2,2,1,32,64]{4,3,2,1,0:T(8,128)S(1)}, u32[]{:S(2)}, u32[]{:S(2)}) collective-permute-start(f32[2,2,1,32,64]{4,3,2,1,0:T(8,128)S(1)} %slice.438), channel_id=1, source_target_pairs={{0,1},{1,2},{2,3},{3,4},{4,5},{5,6},{6,7},{8,9},{9,10},{10,11},{11... | collective-permute-start | bytes 98312 | tf_op jit(solution)/shard_map/ppermute | solution.py:17
  64.9 2.7 collective-permute-start.8
  68.6 4.1 %collective-permute-start.6 = (f32[1,2,4,32,64]{4,3,2,1,0:T(8,128)}, f32[1,2,4,32,64]{4,3,2,1,0:T(8,128)}, u32[]{:S(2)}, u32[]{:S(2)}) collective-permute-start(f32[1,2,4,32,64]{4,3,2,1,0:T(8,128)} %get-tuple-element.45), channel_id=1, source_target_pairs={{0,32},{32,64},{64,96},{96,128},{128,160},{160,192},{192,224},{1,3... | collective-permute-start | bytes 196616 | tf_op jit(solution)/shard_map/ppermute | solution.py:17
  93.8 2.6 collective-permute-start.9
  102.7 2.4 fusion.11
  110.3 5.4 %collective-permute-done.7 = f32[1,2,4,32,64]{4,3,2,1,0:T(8,128)} collective-permute-done((f32[1,2,4,32,64]{4,3,2,1,0:T(8,128)}, f32[1,2,4,32,64]{4,3,2,1,0:T(8,128)}, u32[]{:S(2)}, u32[]{:S(2)}) %collective-permute-start.7) | collective-permute-done | bytes 65568 | tf_op jit(solution)/shard_map/ppermute | solution.py:17
  118.3 2.7 convolution_multiply_fusion
  122.6 4.9 %collective-permute-start.16 = (f32[2,2,1,32,64]{4,3,2,1,0:T(8,128)}, f32[2,2,1,32,64]{4,3,2,1,0:T(8,128)}, u32[]{:S(2)}, u32[]{:S(2)}) collective-permute-start(f32[2,2,1,32,64]{4,3,2,1,0:T(8,128)} %slice.456), channel_id=1, source_target_pairs={{0,1},{1,2},{2,3},{3,4},{4,5},{5,6},{6,7},{8,9},{9,10},{10,11},{11... | collective-permute-start | bytes 98312 | tf_op jit(solution)/shard_map/ppermute | solution.py:17
  129.1 5.0 %collective-permute-start.14 = (f32[2,1,4,32,64]{4,3,2,1,0:T(8,128)}, f32[2,1,4,32,64]{4,3,2,1,0:T(8,128)}, u32[]{:S(2)}, u32[]{:S(2)}) collective-permute-start(f32[2,1,4,32,64]{4,3,2,1,0:T(8,128)} %get-tuple-element.31), channel_id=1, source_target_pairs={{0,8},{8,16},{16,24},{1,9},{9,17},{17,25},{2,10},{10,18},{18,26},{... | collective-permute-start | bytes 196616 | tf_op jit(solution)/shard_map/ppermute | solution.py:17
  135.1 5.2 %collective-permute-start.12 = (f32[1,2,4,32,64]{4,3,2,1,0:T(8,128)}, f32[1,2,4,32,64]{4,3,2,1,0:T(8,128)}, u32[]{:S(2)}, u32[]{:S(2)}) collective-permute-start(f32[1,2,4,32,64]{4,3,2,1,0:T(8,128)} %get-tuple-element.33), channel_id=1, source_target_pairs={{0,32},{32,64},{64,96},{96,128},{128,160},{160,192},{192,224},{1,3... | collective-permute-start | bytes 196616 | tf_op jit(solution)/shard_map/ppermute | solution.py:17
  143.9 2.5 reverse_select_fusion.6
  161.1 2.5 reverse_select_fusion.8
  184.4 2.7 fusion.8
  195.3 3.7 %collective-permute-done.13 = f32[1,2,4,32,64]{4,3,2,1,0:T(8,128)} collective-permute-done((f32[1,2,4,32,64]{4,3,2,1,0:T(8,128)}, f32[1,2,4,32,64]{4,3,2,1,0:T(8,128)}, u32[]{:S(2)}, u32[]{:S(2)}) %collective-permute-start.13) | collective-permute-done | bytes 65568 | tf_op jit(solution)/shard_map/ppermute | solution.py:17
  208.2 4.0 %collective-permute-start.22 = (f32[2,2,1,32,64]{4,3,2,1,0:T(8,128)S(1)}, f32[2,2,1,32,64]{4,3,2,1,0:T(8,128)S(1)}, u32[]{:S(2)}, u32[]{:S(2)}) collective-permute-start(f32[2,2,1,32,64]{4,3,2,1,0:T(8,128)S(1)} %slice.474), channel_id=1, source_target_pairs={{0,1},{1,2},{2,3},{3,4},{4,5},{5,6},{6,7},{8,9},{9,10},{10,11},{11... | collective-permute-start | bytes 98312 | tf_op jit(solution)/shard_map/ppermute | solution.py:17
  213.0 7.2 %collective-permute-start.20 = (f32[2,1,4,32,64]{4,3,2,1,0:T(8,128)S(1)}, f32[2,1,4,32,64]{4,3,2,1,0:T(8,128)}, u32[]{:S(2)}, u32[]{:S(2)}) collective-permute-start(f32[2,1,4,32,64]{4,3,2,1,0:T(8,128)S(1)} %get-tuple-element.19), channel_id=1, source_target_pairs={{0,8},{8,16},{16,24},{1,9},{9,17},{17,25},{2,10},{10,18},{18,26},{... | collective-permute-start | bytes 196616 | tf_op jit(solution)/shard_map/ppermute | solution.py:17
  222.3 4.0 %collective-permute-start.18 = (f32[1,2,4,32,64]{4,3,2,1,0:T(8,128)S(1)}, f32[1,2,4,32,64]{4,3,2,1,0:T(8,128)S(1)}, u32[]{:S(2)}, u32[]{:S(2)}) collective-permute-start(f32[1,2,4,32,64]{4,3,2,1,0:T(8,128)S(1)} %get-tuple-element.21), channel_id=1, source_target_pairs={{0,32},{32,64},{64,96},{96,128},{128,160},{160,192},{192,224},{1,3... | collective-permute-start | bytes 196616 | tf_op jit(solution)/shard_map/ppermute | solution.py:17
  229.9 3.5 %reverse_select_fusion = (f32[2,2,4,32,8,8]{3,5,4,2,1,0:T(8,128)S(1)}, f32[2,2,4,32,8,8]{3,5,4,2,1,0:T(8,128)}, f32[2,2,4,32,8,8]{3,5,4,2,1,0:T(8,128)S(1)}, f32[2,2,4,32,8,8]{3,5,4,2,1,0:T(8,128)}) fusion(f32[2,2,4,32,8,8]{3,5,4,2,1,0:T(8,128)} %bitcast.220, pred[2,2,4]{2,1,0:T(4,128)(4,1)S(1)} %copy-done.62, f32[2,2,4,32,8,8]{3,5,4,2,1,0:T(8,128)} %bitcast.221, ...), kind=kLoop, calls=%fused_computation.9 | loop fusion | flops 131072 | bytes 1048608 | tf_op jit(solution)/shard_map/jit(_where)/select_n | solution.py:23
  262.4 2.4 fusion.5
  270.1 4.2 %collective-permute-done.19 = f32[1,2,4,32,64]{4,3,2,1,0:T(8,128)} collective-permute-done((f32[1,2,4,32,64]{4,3,2,1,0:T(8,128)}, f32[1,2,4,32,64]{4,3,2,1,0:T(8,128)}, u32[]{:S(2)}, u32[]{:S(2)}) %collective-permute-start.19) | collective-permute-done | bytes 65568 | tf_op jit(solution)/shard_map/ppermute | solution.py:17
  (365 shorter events, 180.9 us)
Async XLA Ops:
  2.1 28.4 %collective-permute-start = (f32[1,2,4,32,64]{3,4,2,1,0:T(8,128)}, f32[1,2,4,32,64]{3,4,2,1,0:T(8,128)}, u32[]{:S(2)}, u32[]{:S(2)}) collective-permute-start(f32[1,2,4,32,64]{3,4,2,1,0:T(8,128)} %copy.75), channel_id=1, source_target_pairs={{0,32},{32,64},{64,96},{96,128},{128,160},{160,192},{192,224},{1,3... | collective-permute-start | bytes 196616 | tf_op jit(solution)/shard_map/ppermute | solution.py:17
  8.0 14.5 %collective-permute-start.4 = (f32[2,2,1,32,64]{3,4,2,1,0:T(8,128)}, f32[2,2,1,32,64]{3,4,2,1,0:T(8,128)}, u32[]{:S(2)}, u32[]{:S(2)}) collective-permute-start(f32[2,2,1,32,64]{3,4,2,1,0:T(8,128)} %copy.81), channel_id=1, source_target_pairs={{0,1},{1,2},{2,3},{3,4},{4,5},{5,6},{6,7},{8,9},{9,10},{10,11},{11... | collective-permute-start | bytes 98312 | tf_op jit(solution)/shard_map/ppermute | solution.py:17
  12.7 24.9 %collective-permute-start.2 = (f32[2,1,4,32,64]{3,4,2,1,0:T(8,128)}, f32[2,1,4,32,64]{3,4,2,1,0:T(8,128)}, u32[]{:S(2)}, u32[]{:S(2)}) collective-permute-start(f32[2,1,4,32,64]{3,4,2,1,0:T(8,128)} %copy.77), channel_id=1, source_target_pairs={{0,8},{8,16},{16,24},{1,9},{9,17},{17,25},{2,10},{10,18},{18,26},{... | collective-permute-start | bytes 196616 | tf_op jit(solution)/shard_map/ppermute | solution.py:17
  28.3 12.8 %collective-permute-start.5 = (f32[2,2,1,32,64]{4,3,2,1,0:T(8,128)}, f32[2,2,1,32,64]{4,3,2,1,0:T(8,128)}, u32[]{:S(2)}, u32[]{:S(2)}) collective-permute-start(f32[2,2,1,32,64]{4,3,2,1,0:T(8,128)} %copy.84), channel_id=1, source_target_pairs={{1,0},{2,1},{3,2},{4,3},{5,4},{6,5},{7,6},{9,8},{10,9},{11,10},{12... | collective-permute-start | bytes 98312 | tf_op jit(solution)/shard_map/ppermute | solution.py:17
  36.3 6.0 %collective-permute-start.1 = (f32[1,2,4,32,64]{4,3,2,1,0:T(8,128)}, f32[1,2,4,32,64]{4,3,2,1,0:T(8,128)}, u32[]{:S(2)}, u32[]{:S(2)}) collective-permute-start(f32[1,2,4,32,64]{4,3,2,1,0:T(8,128)} %copy.15), channel_id=1, source_target_pairs={{32,0},{64,32},{96,64},{128,96},{160,128},{192,160},{224,192},{33,... | collective-permute-start | bytes 196616 | tf_op jit(solution)/shard_map/ppermute | solution.py:17
  45.3 7.8 %collective-permute-start.3 = (f32[2,1,4,32,64]{4,3,2,1,0:T(8,128)S(1)}, f32[2,1,4,32,64]{4,3,2,1,0:T(8,128)S(1)}, u32[]{:S(2)}, u32[]{:S(2)}) collective-permute-start(f32[2,1,4,32,64]{4,3,2,1,0:T(8,128)S(1)} %copy.80), channel_id=1, source_target_pairs={{8,0},{16,8},{24,16},{9,1},{17,9},{25,17},{10,2},{18,10},{26,18},{... | collective-permute-start | bytes 196616 | tf_op jit(solution)/shard_map/ppermute | solution.py:17
  59.9 13.7 %collective-permute-start.10 = (f32[2,2,1,32,64]{4,3,2,1,0:T(8,128)S(1)}, f32[2,2,1,32,64]{4,3,2,1,0:T(8,128)S(1)}, u32[]{:S(2)}, u32[]{:S(2)}) collective-permute-start(f32[2,2,1,32,64]{4,3,2,1,0:T(8,128)S(1)} %slice.438), channel_id=1, source_target_pairs={{0,1},{1,2},{2,3},{3,4},{4,5},{5,6},{6,7},{8,9},{9,10},{10,11},{11... | collective-permute-start | bytes 98312 | tf_op jit(solution)/shard_map/ppermute | solution.py:17
  64.9 19.9 %collective-permute-start.8 = (f32[2,1,4,32,64]{4,3,2,1,0:T(8,128)S(1)}, f32[2,1,4,32,64]{4,3,2,1,0:T(8,128)}, u32[]{:S(2)}, u32[]{:S(2)}) collective-permute-start(f32[2,1,4,32,64]{4,3,2,1,0:T(8,128)S(1)} %get-tuple-element.43), channel_id=1, source_target_pairs={{0,8},{8,16},{16,24},{1,9},{9,17},{17,25},{2,10},{10,18},{18,26},{... | collective-permute-start | bytes 196616 | tf_op jit(solution)/shard_map/ppermute | solution.py:17
  68.6 27.8 %collective-permute-start.6 = (f32[1,2,4,32,64]{4,3,2,1,0:T(8,128)}, f32[1,2,4,32,64]{4,3,2,1,0:T(8,128)}, u32[]{:S(2)}, u32[]{:S(2)}) collective-permute-start(f32[1,2,4,32,64]{4,3,2,1,0:T(8,128)} %get-tuple-element.45), channel_id=1, source_target_pairs={{0,32},{32,64},{64,96},{96,128},{128,160},{160,192},{192,224},{1,3... | collective-permute-start | bytes 196616 | tf_op jit(solution)/shard_map/ppermute | solution.py:17
  82.6 20.0 %collective-permute-start.11 = (f32[2,2,1,32,64]{4,3,2,1,0:T(8,128)}, f32[2,2,1,32,64]{4,3,2,1,0:T(8,128)}, u32[]{:S(2)}, u32[]{:S(2)}) collective-permute-start(f32[2,2,1,32,64]{4,3,2,1,0:T(8,128)} %copy.88), channel_id=1, source_target_pairs={{1,0},{2,1},{3,2},{4,3},{5,4},{6,5},{7,6},{9,8},{10,9},{11,10},{12... | collective-permute-start | bytes 98312 | tf_op jit(solution)/shard_map/ppermute | solution.py:17
  93.8 8.8 %collective-permute-start.9 = (f32[2,1,4,32,64]{4,3,2,1,0:T(8,128)}, f32[2,1,4,32,64]{4,3,2,1,0:T(8,128)}, u32[]{:S(2)}, u32[]{:S(2)}) collective-permute-start(f32[2,1,4,32,64]{4,3,2,1,0:T(8,128)} %copy.86), channel_id=1, source_target_pairs={{8,0},{16,8},{24,16},{9,1},{17,9},{25,17},{10,2},{18,10},{26,18},{... | collective-permute-start | bytes 196616 | tf_op jit(solution)/shard_map/ppermute | solution.py:17
  108.2 7.5 %collective-permute-start.7 = (f32[1,2,4,32,64]{4,3,2,1,0:T(8,128)}, f32[1,2,4,32,64]{4,3,2,1,0:T(8,128)}, u32[]{:S(2)}, u32[]{:S(2)}) collective-permute-start(f32[1,2,4,32,64]{4,3,2,1,0:T(8,128)} %copy.32), channel_id=1, source_target_pairs={{32,0},{64,32},{96,64},{128,96},{160,128},{192,160},{224,192},{33,... | collective-permute-start | bytes 196616 | tf_op jit(solution)/shard_map/ppermute | solution.py:17
  122.6 18.7 %collective-permute-start.16 = (f32[2,2,1,32,64]{4,3,2,1,0:T(8,128)}, f32[2,2,1,32,64]{4,3,2,1,0:T(8,128)}, u32[]{:S(2)}, u32[]{:S(2)}) collective-permute-start(f32[2,2,1,32,64]{4,3,2,1,0:T(8,128)} %slice.456), channel_id=1, source_target_pairs={{0,1},{1,2},{2,3},{3,4},{4,5},{5,6},{6,7},{8,9},{9,10},{10,11},{11... | collective-permute-start | bytes 98312 | tf_op jit(solution)/shard_map/ppermute | solution.py:17
  129.1 29.4 %collective-permute-start.14 = (f32[2,1,4,32,64]{4,3,2,1,0:T(8,128)}, f32[2,1,4,32,64]{4,3,2,1,0:T(8,128)}, u32[]{:S(2)}, u32[]{:S(2)}) collective-permute-start(f32[2,1,4,32,64]{4,3,2,1,0:T(8,128)} %get-tuple-element.31), channel_id=1, source_target_pairs={{0,8},{8,16},{16,24},{1,9},{9,17},{17,25},{2,10},{10,18},{18,26},{... | collective-permute-start | bytes 196616 | tf_op jit(solution)/shard_map/ppermute | solution.py:17
  135.1 37.1 %collective-permute-start.12 = (f32[1,2,4,32,64]{4,3,2,1,0:T(8,128)}, f32[1,2,4,32,64]{4,3,2,1,0:T(8,128)}, u32[]{:S(2)}, u32[]{:S(2)}) collective-permute-start(f32[1,2,4,32,64]{4,3,2,1,0:T(8,128)} %get-tuple-element.33), channel_id=1, source_target_pairs={{0,32},{32,64},{64,96},{96,128},{128,160},{160,192},{192,224},{1,3... | collective-permute-start | bytes 196616 | tf_op jit(solution)/shard_map/ppermute | solution.py:17
  156.3 28.1 %collective-permute-start.17 = (f32[2,2,1,32,64]{4,3,2,1,0:T(8,128)}, f32[2,2,1,32,64]{4,3,2,1,0:T(8,128)}, u32[]{:S(2)}, u32[]{:S(2)}) collective-permute-start(f32[2,2,1,32,64]{4,3,2,1,0:T(8,128)} %copy.92), channel_id=1, source_target_pairs={{1,0},{2,1},{3,2},{4,3},{5,4},{6,5},{7,6},{9,8},{10,9},{11,10},{12... | collective-permute-start | bytes 98312 | tf_op jit(solution)/shard_map/ppermute | solution.py:17
  170.2 14.1 %collective-permute-start.15 = (f32[2,1,4,32,64]{4,3,2,1,0:T(8,128)}, f32[2,1,4,32,64]{4,3,2,1,0:T(8,128)}, u32[]{:S(2)}, u32[]{:S(2)}) collective-permute-start(f32[2,1,4,32,64]{4,3,2,1,0:T(8,128)} %copy.90), channel_id=1, source_target_pairs={{8,0},{16,8},{24,16},{9,1},{17,9},{25,17},{10,2},{18,10},{26,18},{... | collective-permute-start | bytes 196616 | tf_op jit(solution)/shard_map/ppermute | solution.py:17
  193.0 6.0 %collective-permute-start.13 = (f32[1,2,4,32,64]{4,3,2,1,0:T(8,128)}, f32[1,2,4,32,64]{4,3,2,1,0:T(8,128)}, u32[]{:S(2)}, u32[]{:S(2)}) collective-permute-start(f32[1,2,4,32,64]{4,3,2,1,0:T(8,128)} %copy.47), channel_id=1, source_target_pairs={{32,0},{64,32},{96,64},{128,96},{160,128},{192,160},{224,192},{33,... | collective-permute-start | bytes 196616 | tf_op jit(solution)/shard_map/ppermute | solution.py:17
  208.2 18.1 %collective-permute-start.22 = (f32[2,2,1,32,64]{4,3,2,1,0:T(8,128)S(1)}, f32[2,2,1,32,64]{4,3,2,1,0:T(8,128)S(1)}, u32[]{:S(2)}, u32[]{:S(2)}) collective-permute-start(f32[2,2,1,32,64]{4,3,2,1,0:T(8,128)S(1)} %slice.474), channel_id=1, source_target_pairs={{0,1},{1,2},{2,3},{3,4},{4,5},{5,6},{6,7},{8,9},{9,10},{10,11},{11... | collective-permute-start | bytes 98312 | tf_op jit(solution)/shard_map/ppermute | solution.py:17
  213.0 14.3 %collective-permute-start.20 = (f32[2,1,4,32,64]{4,3,2,1,0:T(8,128)S(1)}, f32[2,1,4,32,64]{4,3,2,1,0:T(8,128)}, u32[]{:S(2)}, u32[]{:S(2)}) collective-permute-start(f32[2,1,4,32,64]{4,3,2,1,0:T(8,128)S(1)} %get-tuple-element.19), channel_id=1, source_target_pairs={{0,8},{8,16},{16,24},{1,9},{9,17},{17,25},{2,10},{10,18},{18,26},{... | collective-permute-start | bytes 196616 | tf_op jit(solution)/shard_map/ppermute | solution.py:17
  222.3 19.7 %collective-permute-start.18 = (f32[1,2,4,32,64]{4,3,2,1,0:T(8,128)S(1)}, f32[1,2,4,32,64]{4,3,2,1,0:T(8,128)S(1)}, u32[]{:S(2)}, u32[]{:S(2)}) collective-permute-start(f32[1,2,4,32,64]{4,3,2,1,0:T(8,128)S(1)} %get-tuple-element.21), channel_id=1, source_target_pairs={{0,32},{32,64},{64,96},{96,128},{128,160},{160,192},{192,224},{1,3... | collective-permute-start | bytes 196616 | tf_op jit(solution)/shard_map/ppermute | solution.py:17
  240.0 22.3 %collective-permute-start.21 = (f32[2,1,4,32,64]{4,3,2,1,0:T(8,128)}, f32[2,1,4,32,64]{4,3,2,1,0:T(8,128)}, u32[]{:S(2)}, u32[]{:S(2)}) collective-permute-start(f32[2,1,4,32,64]{4,3,2,1,0:T(8,128)} %copy.94), channel_id=1, source_target_pairs={{8,0},{16,8},{24,16},{9,1},{17,9},{25,17},{10,2},{18,10},{26,18},{... | collective-permute-start | bytes 196616 | tf_op jit(solution)/shard_map/ppermute | solution.py:17
  252.5 9.8 %collective-permute-start.23 = (f32[2,2,1,32,64]{4,3,2,1,0:T(8,128)S(1)}, f32[2,2,1,32,64]{4,3,2,1,0:T(8,128)}, u32[]{:S(2)}, u32[]{:S(2)}) collective-permute-start(f32[2,2,1,32,64]{4,3,2,1,0:T(8,128)S(1)} %copy.96), channel_id=1, source_target_pairs={{1,0},{2,1},{3,2},{4,3},{5,4},{6,5},{7,6},{9,8},{10,9},{11,10},{12... | collective-permute-start | bytes 98312 | tf_op jit(solution)/shard_map/ppermute | solution.py:17
  268.0 6.3 %collective-permute-start.19 = (f32[1,2,4,32,64]{4,3,2,1,0:T(8,128)}, f32[1,2,4,32,64]{4,3,2,1,0:T(8,128)}, u32[]{:S(2)}, u32[]{:S(2)}) collective-permute-start(f32[1,2,4,32,64]{4,3,2,1,0:T(8,128)} %copy.62), channel_id=1, source_target_pairs={{32,0},{64,32},{96,64},{128,96},{160,128},{192,160},{224,192},{33,... | collective-permute-start | bytes 196616 | tf_op jit(solution)/shard_map/ppermute | solution.py:17
  (64 other events, 367.8 us)
where the time goes:
time: 283 us; the launch traced here: 278 us
  local copies, waits for them, and re-layouts  103 us (36%)
  starting transfers between devices  74.2 us (26%)
  other arithmetic  65.6 us (23%)
  waiting for transfers between devices  20.3 us (7%)
  matrix products  13.6 us (5%)
    ppermute x24, starting transfers between devices, passed_along(): lax.ppermute(value, axis, [(source, source + steps) for source in range(l...  74.2 us
    rev x24, local copies, waits for them, and re-layouts, flip_face(): reshaped = jnp.where(codes_full // 2 == 1, jnp.flip(reshaped, -1), reshaped)  26.3 us
    unnamed x150, local copies, waits for them, and re-layouts  25.1 us
    reshape x12, other arithmetic, flip_face(): return reshaped.reshape(face_data.shape)  20.5 us
    ppermute x24, waiting for transfers between devices, passed_along(): lax.ppermute(value, axis, [(source, source + steps) for source in range(l...  20.3 us
    select_n x15, other arithmetic, flip_face(): reshaped = jnp.where(codes_full % 2 == 1, jnp.flip(reshaped, -2), reshaped)  15.3 us
    dot_general x15, matrix products, product(): jnp.dot(left, right, precision=lax.Precision.HIGHEST, preferred_element_t...  13.6 us
    mul x8, other arithmetic, one_axis(): (top_face + above) * keep_top[:, :, :, None, None]  13.1 us
  transfers between devices with their start and end apart: 24, of which 5 were waited for; matrix products, arithmetic and copies ran while one was open for 45% of the time, Pallas kernels for 0%

commit v1 on v0

v1 whole, which is shorter than its diff:
```python
import jax
import jax.numpy as jnp
from jax import lax
from jax.experimental import pallas as pl
from jax.experimental.pallas import tpu as pltpu
from jax.sharding import PartitionSpec as P

CYCLES = 2
ROUNDS = 2 * CYCLES
HALVES = 2
AXES = ("ex", "ey", "ez")

fine_weight = 0.5
coarse_weight = 0.5


def parts_of(value):
    high = value.astype(jnp.bfloat16)
    low = (value - high.astype(jnp.float32)).astype(jnp.bfloat16)
    return high, low


def small_dot(left, right):
    left_high, left_low = parts_of(left)
    right_high, right_low = parts_of(right)

    def one(a, b):
        return jnp.dot(a, b, preferred_element_type=jnp.float32)

    return one(left_high, right_high) + one(left_low, right_high) + one(left_high, right_low)


def kernel(
    load_hbm, fine_matrix_hbm, fine_inverse_hbm, scaling_ref, prolong_four_ref, coarse_four_ref, prolong_two_ref,
    coarse_two_ref, orient_ref, boundary_ref,
    out_hbm,
    load_v, out_v, y_v, swapped_v, assembled_v, first_v, matrix_v, operator_v, smoother_v,
    index_v, face_index_v, keep_inverse_v, inverse_v, keep_scale_v, scale_v, keep_v,
    sent_xy, sent_z, got_xy, got_z,
    load_sem, matrix_sem, out_sem, send_sem, recv_sem,
):
    groups = load_v.shape[1] // HALVES
    position = [lax.axis_index(axis) for axis in AXES]
    size = [lax.axis_size(axis) for axis in AXES]
    has_below = [position[a] > 0 for a in range(3)]
    has_above = [position[a] < size[a] - 1 for a in range(3)]

    def load_copy(half):
        rows = pl.ds(half * groups, groups)
        return pltpu.make_async_copy(load_hbm.at[:, rows], load_v.at[:, rows], load_sem.at[half])

    def out_copy(half):
        rows = pl.ds(half * groups, groups)
        return pltpu.make_async_copy(out_v.at[:, rows], out_hbm.at[:, rows], out_sem.at[half])

    fine_inverse_copy = pltpu.make_async_copy(fine_inverse_hbm, matrix_v.at[0], matrix_sem.at[0])
    fine_matrix_copy = pltpu.make_async_copy(fine_matrix_hbm, matrix_v.at[1], matrix_sem.at[1])
    for half in range(HALVES):
        load_copy(half).start()
    fine_inverse_copy.start()
    fine_matrix_copy.start()

    barrier = pltpu.get_barrier_semaphore()
    for a in range(3):
        for there, step in ((has_below[a], -1), (has_above[a], 1)):

            @pl.when(there)
            def _():
                pl.semaphore_signal(
                    barrier, inc=1, device_id={AXES[a]: position[a] + step}, device_id_type=pl.DeviceIdType.MESH
                )

    lane = lax.broadcasted_iota(jnp.int32, (8, 128), 1)
    lower_half = lane < 64

    def mask_of(a, i, j, k):
        code = orient_ref[a, i, j, k]
        return (code & 1) * 56 + (code >> 1) * 7

    for i in range(2):
        for j in range(2):
            for k in range(4):
                e = (i * 2 + j) * 4 + k
                for a in range(3):
                    above = [i, j, k]
                    above[a] += 1
                    own = mask_of(a, i, j, k)
                    if above[a] < (2, 2, 4)[a]:
                        bits = jnp.where(lower_half, mask_of(a, *above), own)
                    else:
                        bits = jnp.full((8, 128), own, jnp.int32)
                    index_v[a, e] = (lane ^ 64) ^ bits
                    if (i, j, k)[a] == 0:
                        parity = j if a == 2 else k % 2
                        slot = (j * 4 + k, i * 4 + k, i * 2 + j)[a]
                        face_index_v[a, slot] = lane ^ (own ^ (64 * parity))

                row = jnp.broadcast_to(scaling_ref[i, j, k : k + 1, :], (8, scaling_ref.shape[-1]))
                inverse = 1.0 / row
                keeps = []
                for a in range(3):
                    low_zero = jnp.where((i, j, k)[a] == 0, jnp.where(position[a] == 0, boundary_ref[i, j, k, 2 * a], 0), 0)
                    at_top = (i, j, k)[a] == (2, 2, 4)[a] - 1
                    top_zero = jnp.where(at_top, jnp.where(position[a] == size[a] - 1, boundary_ref[i, j, k, 2 * a + 1], 0), 0)
                    keeps.append((1 - jnp.where(lower_half, low_zero, top_zero)).astype(jnp.float32))
                keep = jnp.concatenate(keeps, -1)
                scale_v[e] = row
                inverse_v[e] = inverse
                keep_scale_v[e] = keep * row
                keep_inverse_v[e] = keep * inverse
                keep_v[e] = keep

    for a in range(3):
        for there, direction in ((has_above[a], 0), (has_below[a], 1)):

            @pl.when(jnp.logical_not(there))
            def _():
                for turn in range(ROUNDS):
                    for half in range(HALVES):
                        if a < 2:
                            got_xy[turn, half, 2 * a + direction] = jnp.zeros(got_xy.shape[3:], jnp.float32)
                        else:
                            got_z[turn, half, direction] = jnp.zeros(got_z.shape[3:], jnp.float32)

    def face_copy(turn, half, a, direction):
        channel = 2 * a + direction
        if a < 2:
            source, target = sent_xy.at[turn, half, channel], got_xy.at[turn, half, channel]
        else:
            source, target = sent_z.at[turn, half, direction], got_z.at[turn, half, direction]
        return pltpu.make_async_remote_copy(
            source, target, send_sem.at[turn, half, channel], recv_sem.at[turn, half, channel],
            device_id={AXES[a]: position[a] + (1 if direction else -1)}, device_id_type=pl.DeviceIdType.MESH,
        )

    def rolled(value):
        return pltpu.roll(value.reshape(-1, 128), 64, 1).reshape(value.shape)

    def gathered(value, index):
        index = jnp.broadcast_to(index, value.shape)
        return jnp.take_along_axis(
            value.reshape(-1, 128), index.reshape(-1, 128), axis=1, mode="promise_in_bounds"
        ).reshape(value.shape)

    def edge(value, a, last):
        layer = lax.index_in_dim(value, -1 if last else 0, a, keepdims=False)
        if a < 2:
            layer = layer.reshape((2, 2, 2) + layer.shape[2:])
            return layer[:, :, 0], layer[:, :, 1]
        return layer[:, 0], layer[:, 1]

    def packed(pair):
        first, second = pair
        return jnp.where(lower_half, rolled(first), second)

    def shaped(value):
        return value.reshape((2, 2, 4) + value.shape[1:])

    def send(turn, half, source, a):
        swapped = gathered(source, index_v[a][:, None])
        swapped_v[half, a] = swapped
        down = packed(edge(shaped(swapped), a, False))
        up = packed(edge(shaped(source), a, True))
        if a < 2:
            sent_xy[turn, half, 2 * a] = down.reshape(sent_xy.shape[3:])
            sent_xy[turn, half, 2 * a + 1] = up.reshape(sent_xy.shape[3:])
        else:
            sent_z[turn, half, 0] = down.reshape(sent_z.shape[3:])
            sent_z[turn, half, 1] = up.reshape(sent_z.shape[3:])
        for there, direction in ((has_below[a], 0), (has_above[a], 1)):

            @pl.when(there)
            def _():
                face_copy(turn, half, a, direction).start()

    def receive(turn, half):
        for a in range(3):

            @pl.when(has_below[a])
            def _():
                face_copy(turn, half, a, 0).wait_send()
                face_copy(turn, half, a, 1).wait_recv()

            @pl.when(has_above[a])
            def _():
                face_copy(turn, half, a, 1).wait_send()
                face_copy(turn, half, a, 0).wait_recv()

    def assembled_sum(turn, half, source, a):
        swapped = shaped(swapped_v[half, a])
        if a < 2:
            down, up = got_xy[turn, half, 2 * a], got_xy[turn, half, 2 * a + 1]
            lead = (2, 2)
        else:
            down, up = got_z[turn, half, 0], got_z[turn, half, 1]
            lead = (2,)
        face_index = face_index_v[a, : 4 if a == 2 else 8].reshape(lead + (2, 8, 128))
        wide = lead + down.shape[1:]
        down, up = down.reshape(wide), up.reshape(wide)
        top = jnp.stack([rolled(down), down], len(lead))
        low = jnp.stack(
            [gathered(up, lax.index_in_dim(face_index, parity, len(lead), keepdims=True)) for parity in range(2)],
            len(lead),
        )
        layer = list(swapped.shape)
        layer[a] = 1
        top, low = top.reshape(layer), low.reshape(layer)
        count = swapped.shape[a]
        from_below = jnp.concatenate([low, lax.slice_in_dim(swapped, 0, count - 1, axis=a)], a)
        from_above = jnp.concatenate([lax.slice_in_dim(swapped, 1, count, axis=a), top], a)
        return source + jnp.where(lower_half, from_below, from_above).reshape(source.shape)

    def columns(a):
        return slice(a * 128, (a + 1) * 128)

    def multiply_and_send(turn, half, row_parts, matrix_ref, factor_ref):
        high, low = (jnp.concatenate(parts, -1) for parts in zip(*row_parts))
        rows = jnp.concatenate([high, low, high], -1)
        for span in ((0, 2), (2, 3)):
            wide = slice(span[0] * 128, span[1] * 128)
            out = jnp.dot(rows, matrix_ref[:, wide], preferred_element_type=jnp.float32)
            for a in range(*span):
                piece = out[:, (a - span[0]) * 128 : (a - span[0] + 1) * 128].reshape(16, groups, 8, 128)
                piece = piece * factor_ref[:, :, columns(a)][:, None]
                y_v[half, a] = piece
                send(turn, half, piece, a)

    def half_rows(ref, half, a):
        return ref[:, half * groups : (half + 1) * groups, :, columns(a)]

    pl.semaphore_wait(barrier, sum(there.astype(jnp.int32) for there in has_below + has_above))

    for half in range(HALVES):
        load_copy(half).wait()
        for a in range(3):
            send(0, half, half_rows(load_v, half, a), a)

    coarse = small_dot(
        prolong_four_ref[...].T, small_dot(coarse_four_ref[...], prolong_four_ref[...])
    ) + small_dot(prolong_two_ref[...].T, small_dot(coarse_two_ref[...], prolong_two_ref[...]))
    fine_inverse_copy.wait()
    smoother_high, smoother_low = parts_of(fine_weight * matrix_v[0] + coarse_weight * coarse)
    nodes = smoother_high.shape[0]
    smoother_v[:nodes] = smoother_high
    smoother_v[nodes : 2 * nodes] = smoother_high
    smoother_v[2 * nodes :] = smoother_low
    fine_matrix_copy.wait()
    operator_high, operator_low = parts_of(matrix_v[1])
    operator_v[:nodes] = operator_high
    operator_v[nodes : 2 * nodes] = operator_high
    operator_v[2 * nodes :] = operator_low

    def flat_parts(value):
        return parts_of(value.reshape(-1, 128))

    for half in range(HALVES):
        receive(0, half)
        row_parts = []
        for a in range(3):
            total = assembled_sum(0, half, half_rows(load_v, half, a), a)
            assembled_v[half, a] = total
            row_parts.append(flat_parts(total * keep_inverse_v[:, :, columns(a)][:, None]))
        multiply_and_send(1, half, row_parts, smoother_v, inverse_v)
    for half in range(HALVES):
        receive(1, half)
        row_parts = []
        for a in range(3):
            total = assembled_sum(1, half, y_v[half, a], a)
            first_v[half, a] = total
            row_parts.append(flat_parts(total * keep_scale_v[:, :, columns(a)][:, None]))
        multiply_and_send(2, half, row_parts, operator_v, scale_v)
    for half in range(HALVES):
        receive(2, half)
        row_parts = []
        for a in range(3):
            total = assembled_v[half, a] - assembled_sum(2, half, y_v[half, a], a)
            row_parts.append(flat_parts(total * keep_inverse_v[:, :, columns(a)][:, None]))
        multiply_and_send(3, half, row_parts, smoother_v, inverse_v)
    for half in range(HALVES):
        receive(3, half)
        for a in range(3):
            total = first_v[half, a] + assembled_sum(3, half, y_v[half, a], a)
            out_v[:, half * groups : (half + 1) * groups, :, columns(a)] = total * keep_v[:, :, columns(a)][:, None]
        out_copy(half).start()
    for half in range(HALVES):
        out_copy(half).wait()


def body(
    load_raw, scaling, fine_matrix, fine_inverse, prolong_four, coarse_four, prolong_two, coarse_two, orient, boundary
):
    nodes = load_raw.shape[-1]
    groups = load_raw.shape[3] // 8
    local = groups // HALVES
    elements = 16
    f32, bf16 = jnp.float32, jnp.bfloat16
    vmem = pl.BlockSpec(memory_space=pltpu.VMEM)
    smem = pl.BlockSpec(memory_space=pltpu.SMEM)
    anywhere = pl.BlockSpec(memory_space=pl.ANY)
    per_half = pltpu.VMEM((HALVES, 3, elements, local, 8, 128), f32)
    factor = pltpu.VMEM((elements, 8, nodes), f32)
    out = pl.pallas_call(
        kernel,
        out_shape=jax.ShapeDtypeStruct((elements, groups, 8, nodes), f32),
        in_specs=[anywhere] * 3 + [vmem] * 5 + [smem] * 2,
        out_specs=anywhere,
        scratch_shapes=[
            pltpu.VMEM((elements, groups, 8, nodes), f32),
            pltpu.VMEM((elements, groups, 8, nodes), f32),
            per_half, per_half, per_half, per_half,
            pltpu.VMEM((2, nodes, nodes), f32),
            pltpu.VMEM((3 * nodes, nodes), bf16),
            pltpu.VMEM((3 * nodes, nodes), bf16),
            pltpu.VMEM((3, elements, 8, 128), jnp.int32),
            pltpu.VMEM((3, 8, 8, 128), jnp.int32),
            factor, factor, factor, factor, factor,
            pltpu.VMEM((ROUNDS, HALVES, 4, 4, local, 8, 128), f32),
            pltpu.VMEM((ROUNDS, HALVES, 2, 2, local, 8, 128), f32),
            pltpu.VMEM((ROUNDS, HALVES, 4, 4, local, 8, 128), f32),
            pltpu.VMEM((ROUNDS, HALVES, 2, 2, local, 8, 128), f32),
            pltpu.SemaphoreType.DMA((HALVES,)),
            pltpu.SemaphoreType.DMA((2,)),
            pltpu.SemaphoreType.DMA((HALVES,)),
            pltpu.SemaphoreType.DMA((ROUNDS, HALVES, 6)),
            pltpu.SemaphoreType.DMA((ROUNDS, HALVES, 6)),
        ],
        compiler_params=pltpu.CompilerParams(collective_id=0, has_side_effects=True),
    )(
        load_raw.reshape(elements, groups, 8, nodes), fine_matrix, fine_inverse, scaling, prolong_four.T, coarse_four,
        prolong_two.T, coarse_two, orient, boundary.transpose(1, 2, 3, 0),
    )
    return out.reshape(load_raw.shape)


def solution(mesh):
    in_specs = (
        P("ex", "ey", "ez", None, None),
        P("ex", "ey", "ez", None),
        P(),
        P(),
        P(),
        P(),
        P(),
        P(),
        P(None, "ex", "ey", "ez"),
        P(None, "ex", "ey", "ez"),
    )
    out_specs = P("ex", "ey", "ez", None, None)
    return jax.shard_map(body, mesh=mesh, in_specs=in_specs, out_specs=out_specs, check_vma=False)
```

time: 283 us -> 29.5 us (0.10); the launches traced: 278 us -> 29.4 us
  local copies, waits for them, and re-layouts: 103 us -> 2.07 us
  starting transfers between devices: 74.2 us -> 0 us
  other arithmetic: 65.6 us -> 0 us
  Pallas kernels: 0 us -> 27.3 us
  waiting for transfers between devices: 20.3 us -> 0 us
  matrix products: 13.6 us -> 0 us
    ppermute x24 -> x0, starting transfers between devices: 74.2 us -> none  [passed_along(): lax.ppermute(value, axis, [(source, source + steps) for source in range(l...]
    slice x57 -> x0, local copies, waits for them, and re-layouts: 27.9 us -> none  [the longest x16 8.53 us: assemble(): element_data[..., face_index * face_nodes:(face_index + 1) * face_nodes]]
    pallas_call x0 -> x1, Pallas kernels: none -> 27.3 us  [body(): pl.pallas_call(kernel, out_shape=jax.ShapeDtypeStruct((elements, groups,...]
    rev x24 -> x0, local copies, waits for them, and re-layouts: 26.3 us -> none  [flip_face(): reshaped = jnp.where(codes_full // 2 == 1, jnp.flip(reshaped, -1), reshaped)]
    reshape x15 -> x0, other arithmetic: 23.4 us -> none  [the longest x12 20.5 us: flip_face(): return reshaped.reshape(face_data.shape)]
    unnamed x150 -> x1, local copies, waits for them, and re-layouts: 25.1 us -> 2.07 us
    ppermute x24 -> x0, waiting for transfers between devices: 20.3 us -> none  [passed_along(): lax.ppermute(value, axis, [(source, source + steps) for source in range(l...]
    select_n x19 -> x0, other arithmetic: 20.2 us -> none  [the longest x15 15.3 us: flip_face(): reshaped = jnp.where(codes_full % 2 == 1, jnp.flip(reshaped, -2), reshaped)]
  transfers between devices with their start and end apart: 24 -> 0, of which waited for: 5 -> 0; matrix products, arithmetic and copies ran while one was open for 45% -> 0% of each run, Pallas kernels for 0% -> 0%
where the time goes in v1:
time: 29.5 us; the launch traced here: 29.4 us
  Pallas kernels  27.3 us (93%)
  local copies, waits for them, and re-layouts  2.07 us (7%)
    pallas_call x1, Pallas kernels, body(): pl.pallas_call(kernel, out_shape=jax.ShapeDtypeStruct((elements, groups,...  27.3 us
    unnamed x1, local copies, waits for them, and re-layouts  2.07 us

profile of v1, /device:TPU:1, one launch (start us, length us, event | category | flops | bytes accessed | tf_op | source)
XLA Modules:
  0.0 29.4 jit_solution(6430101271029234780)
XLA Ops:
  0.0 27.3 %shard_map.100 = f32[16,4,8,384]{3,2,1,0:T(8,128)} custom-call(f32[16,4,8,384]{3,2,1,0:T(8,128)} %bitcast.6, f32[384,384]{1,0:T(8,128)} %fine_matrix_hbm.1, f32[384,384]{1,0:T(8,128)} %fine_inverse_hbm.1, f32[2,2,4,384]{3,2,1,0:T(4,128)} %scaling_ref.1, f32[98,384]{1,0:T(8,128)} %bitcast.7, f32[98,98]{1,0:T(8,128)} %coarse_four_ref.1, f32[26,384]{1,0:T(8,128)} %bitcast.8, ...), custom_call_target="tpu_custom_call" | custom-call | tf_op jit(solution)/shard_map/pallas_call | solution.py:302
  27.3 2.1 %copy.12 = f32[2,2,4,32,384]{4,3,2,1,0:T(8,128)} copy(f32[2,2,4,32,384]{4,3,2,1,0:T(8,128)} %bitcast.5) | data formatting | bytes 1572864

commit v2 on v1

--- a/solution.py
+++ b/solution.py
@@ -9,6 +9,7 @@
 ROUNDS = 2 * CYCLES
 HALVES = 2
 AXES = ("ex", "ey", "ez")
+GROUPS = ((0, 1, 2),)
 
 fine_weight = 0.5
 coarse_weight = 0.5
@@ -31,13 +32,14 @@
 
 
 def kernel(
-    load_hbm, fine_matrix_hbm, fine_inverse_hbm, scaling_ref, prolong_four_ref, coarse_four_ref, prolong_two_ref,
-    coarse_two_ref, orient_ref, boundary_ref,
-    out_hbm,
-    load_v, out_v, y_v, swapped_v, assembled_v, first_v, matrix_v, operator_v, smoother_v,
+    load_hbm, fine_matrix_hbm, fine_inverse_hbm, scaling_hbm, prolong_four_hbm, coarse_four_hbm, prolong_two_hbm,
+    coarse_two_hbm, orient_hbm, boundary_hbm,
+    out_ref,
+    load_v, y_v, swapped_v, assembled_v, first_v, matrix_v, operator_v, smoother_v,
+    scaling_ref, prolong_four_ref, coarse_four_ref, prolong_two_ref, coarse_two_ref, orient_ref, boundary_ref,
     index_v, face_index_v, keep_inverse_v, inverse_v, keep_scale_v, scale_v, keep_v,
     sent_xy, sent_z, got_xy, got_z,
-    load_sem, matrix_sem, out_sem, send_sem, recv_sem,
+    load_sem, small_sem, send_sem, recv_sem,
 ):
     groups = load_v.shape[1] // HALVES
     position = [lax.axis_index(axis) for axis in AXES]
@@ -49,17 +51,6 @@
         rows = pl.ds(half * groups, groups)
         return pltpu.make_async_copy(load_hbm.at[:, rows], load_v.at[:, rows], load_sem.at[half])
 
-    def out_copy(half):
-        rows = pl.ds(half * groups, groups)
-        return pltpu.make_async_copy(out_v.at[:, rows], out_hbm.at[:, rows], out_sem.at[half])
-
-    fine_inverse_copy = pltpu.make_async_copy(fine_inverse_hbm, matrix_v.at[0], matrix_sem.at[0])
-    fine_matrix_copy = pltpu.make_async_copy(fine_matrix_hbm, matrix_v.at[1], matrix_sem.at[1])
-    for half in range(HALVES):
-        load_copy(half).start()
-    fine_inverse_copy.start()
-    fine_matrix_copy.start()
-
     barrier = pltpu.get_barrier_semaphore()
     for a in range(3):
         for there, step in ((has_below[a], -1), (has_above[a], 1)):
@@ -70,8 +61,32 @@
                     barrier, inc=1, device_id={AXES[a]: position[a] + step}, device_id_type=pl.DeviceIdType.MESH
                 )
 
+    small = [
+        pltpu.make_async_copy(source, target, small_sem.at[n])
+        for n, (source, target) in enumerate(
+            (
+                (orient_hbm, orient_ref),
+                (boundary_hbm, boundary_ref),
+                (scaling_hbm, scaling_ref),
+                (coarse_four_hbm, coarse_four_ref),
+                (prolong_four_hbm, prolong_four_ref),
+                (coarse_two_hbm, coarse_two_ref),
+                (prolong_two_hbm, prolong_two_ref),
+                (fine_inverse_hbm, matrix_v.at[0]),
+                (fine_matrix_hbm, matrix_v.at[1]),
+            )
+        )
+    ]
+    small[0].start()
+    for half in range(HALVES):
+        load_copy(half).start()
+    for copy in small[1:]:
+        copy.start()
+
     lane = lax.broadcasted_iota(jnp.int32, (8, 128), 1)
     lower_half = lane < 64
+
+    small[0].wait()
 
     def mask_of(a, i, j, k):
         code = orient_ref[a, i, j, k]
@@ -88,27 +103,12 @@
                     if above[a] < (2, 2, 4)[a]:
                         bits = jnp.where(lower_half, mask_of(a, *above), own)
                     else:
-                        bits = jnp.full((8, 128), own, jnp.int32)
+                        bits = jnp.where(lower_half, 0, own)
                     index_v[a, e] = (lane ^ 64) ^ bits
                     if (i, j, k)[a] == 0:
                         parity = j if a == 2 else k % 2
                         slot = (j * 4 + k, i * 4 + k, i * 2 + j)[a]
                         face_index_v[a, slot] = lane ^ (own ^ (64 * parity))
-
-                row = jnp.broadcast_to(scaling_ref[i, j, k : k + 1, :], (8, scaling_ref.shape[-1]))
-                inverse = 1.0 / row
-                keeps = []
-                for a in range(3):
-                    low_zero = jnp.where((i, j, k)[a] == 0, jnp.where(position[a] == 0, boundary_ref[i, j, k, 2 * a], 0), 0)
-                    at_top = (i, j, k)[a] == (2, 2, 4)[a] - 1
-                    top_zero = jnp.where(at_top, jnp.where(position[a] == size[a] - 1, boundary_ref[i, j, k, 2 * a + 1], 0), 0)
-                    keeps.append((1 - jnp.where(lower_half, low_zero, top_zero)).astype(jnp.float32))
-                keep = jnp.concatenate(keeps, -1)
-                scale_v[e] = row
-                inverse_v[e] = inverse
-                keep_scale_v[e] = keep * row
-                keep_inverse_v[e] = keep * inverse
-                keep_v[e] = keep
 
     for a in range(3):
         for there, direction in ((has_above[a], 0), (has_below[a], 1)):
@@ -149,24 +149,23 @@
             return layer[:, :, 0], layer[:, :, 1]
         return layer[:, 0], layer[:, 1]
 
-    def packed(pair):
-        first, second = pair
-        return jnp.where(lower_half, rolled(first), second)
-
     def shaped(value):
         return value.reshape((2, 2, 4) + value.shape[1:])
 
-    def send(turn, half, source, a):
+    def pack(turn, half, source, a):
         swapped = gathered(source, index_v[a][:, None])
         swapped_v[half, a] = swapped
-        down = packed(edge(shaped(swapped), a, False))
-        up = packed(edge(shaped(source), a, True))
+        first, second = edge(shaped(swapped), a, False)
+        down = jnp.where(lower_half, rolled(first), second)
+        up = jnp.where(lower_half, edge(shaped(swapped), a, True)[0], edge(shaped(source), a, True)[1])
         if a < 2:
             sent_xy[turn, half, 2 * a] = down.reshape(sent_xy.shape[3:])
             sent_xy[turn, half, 2 * a + 1] = up.reshape(sent_xy.shape[3:])
         else:
             sent_z[turn, half, 0] = down.reshape(sent_z.shape[3:])
             sent_z[turn, half, 1] = up.reshape(sent_z.shape[3:])
+
+    def send(turn, half, a):
         for there, direction in ((has_below[a], 0), (has_above[a], 1)):
 
             @pl.when(there)
@@ -214,16 +213,26 @@
         return slice(a * 128, (a + 1) * 128)
 
     def multiply_and_send(turn, half, row_parts, matrix_ref, factor_ref):
-        high, low = (jnp.concatenate(parts, -1) for parts in zip(*row_parts))
-        rows = jnp.concatenate([high, low, high], -1)
-        for span in ((0, 2), (2, 3)):
-            wide = slice(span[0] * 128, span[1] * 128)
-            out = jnp.dot(rows, matrix_ref[:, wide], preferred_element_type=jnp.float32)
-            for a in range(*span):
-                piece = out[:, (a - span[0]) * 128 : (a - span[0] + 1) * 128].reshape(16, groups, 8, 128)
-                piece = piece * factor_ref[:, :, columns(a)][:, None]
+        rows = jnp.concatenate([part for parts in row_parts for part in parts], -1)
+        for group in GROUPS:
+            for a in group:
+                out = jnp.dot(rows, matrix_ref[a], preferred_element_type=jnp.float32)
+                out = out[:, :128] + out[:, 128:]
+                piece = out.reshape(16, groups, 8, 128) * factor_ref[:, :, columns(a)][:, None]
                 y_v[half, a] = piece
-                send(turn, half, piece, a)
+                pack(turn, half, piece, a)
+            for a in group:
+                send(turn, half, a)
+
+    def set_matrix(value, matrix_ref):
+        high, low = parts_of(value)
+        for a in range(3):
+            for b in range(3):
+                block = jnp.concatenate(
+                    [part[b * 128 : (b + 1) * 128, a * 128 : (a + 1) * 128] for part in (high, low)], -1
+                )
+                matrix_ref[a, 2 * b * 128 : (2 * b + 1) * 128] = block
+                matrix_ref[a, (2 * b + 1) * 128 : (2 * b + 2) * 128] = block
 
     def half_rows(ref, half, a):
         return ref[:, half * groups : (half + 1) * groups, :, columns(a)]
@@ -233,22 +242,39 @@
     for half in range(HALVES):
         load_copy(half).wait()
         for a in range(3):
-            send(0, half, half_rows(load_v, half, a), a)
-
+            pack(0, half, half_rows(load_v, half, a), a)
+        for a in range(3):
+            send(0, half, a)
+
+    small[1].wait()
+    small[2].wait()
+    for i in range(2):
+        for j in range(2):
+            for k in range(4):
+                e = (i * 2 + j) * 4 + k
+                row = jnp.broadcast_to(scaling_ref[i, j, k : k + 1, :], (8, scaling_ref.shape[-1]))
+                inverse = 1.0 / row
+                keeps = []
+                for a in range(3):
+                    low_zero = jnp.where((i, j, k)[a] == 0, jnp.where(position[a] == 0, boundary_ref[i, j, k, 2 * a], 0), 0)
+                    at_top = (i, j, k)[a] == (2, 2, 4)[a] - 1
+                    top_zero = jnp.where(at_top, jnp.where(position[a] == size[a] - 1, boundary_ref[i, j, k, 2 * a + 1], 0), 0)
+                    keeps.append((1 - jnp.where(lower_half, low_zero, top_zero)).astype(jnp.float32))
+                keep = jnp.concatenate(keeps, -1)
+                scale_v[e] = row
+                inverse_v[e] = inverse
+                keep_scale_v[e] = keep * row
+                keep_inverse_v[e] = keep * inverse
+                keep_v[e] = keep
+
+    for copy in small[3:8]:
+        copy.wait()
     coarse = small_dot(
         prolong_four_ref[...].T, small_dot(coarse_four_ref[...], prolong_four_ref[...])
     ) + small_dot(prolong_two_ref[...].T, small_dot(coarse_two_ref[...], prolong_two_ref[...]))
-    fine_inverse_copy.wait()
-    smoother_high, smoother_low = parts_of(fine_weight * matrix_v[0] + coarse_weight * coarse)
-    nodes = smoother_high.shape[0]
-    smoother_v[:nodes] = smoother_high
-    smoother_v[nodes : 2 * nodes] = smoother_high
-    smoother_v[2 * nodes :] = smoother_low
-    fine_matrix_copy.wait()
-    operator_high, operator_low = parts_of(matrix_v[1])
-    operator_v[:nodes] = operator_high
-    operator_v[nodes : 2 * nodes] = operator_high
-    operator_v[2 * nodes :] = operator_low
+    set_matrix(fine_weight * matrix_v[0] + coarse_weight * coarse, smoother_v)
+    small[8].wait()
+    set_matrix(matrix_v[1], operator_v)
 
     def flat_parts(value):
         return parts_of(value.reshape(-1, 128))
@@ -280,10 +306,7 @@
         receive(3, half)
         for a in range(3):
             total = first_v[half, a] + assembled_sum(3, half, y_v[half, a], a)
-            out_v[:, half * groups : (half + 1) * groups, :, columns(a)] = total * keep_v[:, :, columns(a)][:, None]
-        out_copy(half).start()
-    for half in range(HALVES):
-        out_copy(half).wait()
+            out_ref[:, half * groups : (half + 1) * groups, :, columns(a)] = total * keep_v[:, :, columns(a)][:, None]
 
 
 def body(
@@ -294,23 +317,26 @@
     local = groups // HALVES
     elements = 16
     f32, bf16 = jnp.float32, jnp.bfloat16
-    vmem = pl.BlockSpec(memory_space=pltpu.VMEM)
-    smem = pl.BlockSpec(memory_space=pltpu.SMEM)
-    anywhere = pl.BlockSpec(memory_space=pl.ANY)
     per_half = pltpu.VMEM((HALVES, 3, elements, local, 8, 128), f32)
     factor = pltpu.VMEM((elements, 8, nodes), f32)
     out = pl.pallas_call(
         kernel,
-        out_shape=jax.ShapeDtypeStruct((elements, groups, 8, nodes), f32),
-        in_specs=[anywhere] * 3 + [vmem] * 5 + [smem] * 2,
-        out_specs=anywhere,
+        out_shape=pltpu.VMEM((elements, groups, 8, nodes), f32),
+        in_specs=[pl.BlockSpec(memory_space=pltpu.HBM)] * 10,
+        out_specs=pl.BlockSpec(memory_space=pltpu.VMEM),
         scratch_shapes=[
-            pltpu.VMEM((elements, groups, 8, nodes), f32),
             pltpu.VMEM((elements, groups, 8, nodes), f32),
             per_half, per_half, per_half, per_half,
             pltpu.VMEM((2, nodes, nodes), f32),
-            pltpu.VMEM((3 * nodes, nodes), bf16),
-            pltpu.VMEM((3 * nodes, nodes), bf16),
+            pltpu.VMEM((3, 2 * nodes, 256), bf16),
+            pltpu.VMEM((3, 2 * nodes, 256), bf16),
+            pltpu.VMEM(scaling.shape, f32),
+            pltpu.VMEM(prolong_four.shape[::-1], f32),
+            pltpu.VMEM(coarse_four.shape, f32),
+            pltpu.VMEM(prolong_two.shape[::-1], f32),
+            pltpu.VMEM(coarse_two.shape, f32),
+            pltpu.SMEM(orient.shape, jnp.int32),
+            pltpu.SMEM(boundary.shape[1:] + boundary.shape[:1], jnp.int32),
             pltpu.VMEM((3, elements, 8, 128), jnp.int32),
             pltpu.VMEM((3, 8, 8, 128), jnp.int32),
             factor, factor, factor, factor, factor,
@@ -319,16 +345,15 @@
             pltpu.VMEM((ROUNDS, HALVES, 4, 4, local, 8, 128), f32),
             pltpu.VMEM((ROUNDS, HALVES, 2, 2, local, 8, 128), f32),
             pltpu.SemaphoreType.DMA((HALVES,)),
-            pltpu.SemaphoreType.DMA((2,)),
-            pltpu.SemaphoreType.DMA((HALVES,)),
+            pltpu.SemaphoreType.DMA((9,)),
             pltpu.SemaphoreType.DMA((ROUNDS, HALVES, 6)),
             pltpu.SemaphoreType.DMA((ROUNDS, HALVES, 6)),
         ],
-        compiler_params=pltpu.CompilerParams(collective_id=0, has_side_effects=True),
-    )(
+        compiler_params=pltpu.CompilerParams(collective_id=0, has_side_effects=True, vmem_limit_bytes=32 * 1024 * 1024),
+    )(*(pltpu.with_memory_space_constraint(value, pltpu.HBM) for value in (
         load_raw.reshape(elements, groups, 8, nodes), fine_matrix, fine_inverse, scaling, prolong_four.T, coarse_four,
         prolong_two.T, coarse_two, orient, boundary.transpose(1, 2, 3, 0),
-    )
+    )))
     return out.reshape(load_raw.shape)
 
 

time: 29.5 us -> 25.8 us (0.87)
  Pallas kernels: 27.3 us -> 24.8 us
  local copies, waits for them, and re-layouts: 2.07 us -> 0.88 us
    pallas_call x1, Pallas kernels: 27.3 us -> 24.8 us  [body(): pl.pallas_call(kernel, out_shape=pltpu.VMEM((elements, groups, 8, nodes),...]
    unnamed x1, local copies, waits for them, and re-layouts: 2.07 us -> 0.88 us
where the time goes in v2:
time: 25.8 us; the launch traced here: 25.7 us
  Pallas kernels  24.8 us (96%)
  local copies, waits for them, and re-layouts  0.88 us (3%)
    pallas_call x1, Pallas kernels, body(): pl.pallas_call(kernel, out_shape=pltpu.VMEM((elements, groups, 8, nodes),...  24.8 us
    unnamed x1, local copies, waits for them, and re-layouts  0.88 us

profile of v2, /device:TPU:1, one launch (start us, length us, event | category | flops | bytes accessed | tf_op | source)
XLA Modules:
  0.0 25.7 jit_solution(14077323061953585151)
XLA Ops:
  0.0 24.8 %shard_map.100 = f32[16,4,8,384]{3,2,1,0:T(8,128)S(1)} custom-call(f32[16,4,8,384]{3,2,1,0:T(8,128)} %bitcast.6, f32[384,384]{1,0:T(8,128)} %fine_matrix_hbm.1, f32[384,384]{1,0:T(8,128)} %fine_inverse_hbm.1, f32[2,2,4,384]{3,2,1,0:T(4,128)} %scaling_hbm.1, f32[98,384]{1,0:T(8,128)} %bitcast.7, f32[98,98]{1,0:T(8,128)} %coarse_four_hbm.1, ...), custom_call_target="tpu_custom_call" | custom-call | tf_op jit(solution)/shard_map/pallas_call | solution.py:322
  24.8 0.9 %copy.12 = f32[2,2,4,32,384]{4,3,2,1,0:T(8,128)} copy(f32[2,2,4,32,384]{4,3,2,1,0:T(8,128)S(1)} %bitcast.5) | data formatting | bytes 1572864

commit v3 on v2

--- a/solution.py
+++ b/solution.py
@@ -9,7 +9,7 @@
 ROUNDS = 2 * CYCLES
 HALVES = 2
 AXES = ("ex", "ey", "ez")
-GROUPS = ((0, 1, 2),)
+ORDER = (1, 0, 2)
 
 fine_weight = 0.5
 coarse_weight = 0.5
@@ -35,7 +35,7 @@
     load_hbm, fine_matrix_hbm, fine_inverse_hbm, scaling_hbm, prolong_four_hbm, coarse_four_hbm, prolong_two_hbm,
     coarse_two_hbm, orient_hbm, boundary_hbm,
     out_ref,
-    load_v, y_v, swapped_v, assembled_v, first_v, matrix_v, operator_v, smoother_v,
+    load_v, y_v, local_v, assembled_v, first_v, matrix_v, operator_v, smoother_v,
     scaling_ref, prolong_four_ref, coarse_four_ref, prolong_two_ref, coarse_two_ref, orient_ref, boundary_ref,
     index_v, face_index_v, keep_inverse_v, inverse_v, keep_scale_v, scale_v, keep_v,
     sent_xy, sent_z, got_xy, got_z,
@@ -80,9 +80,6 @@
     small[0].start()
     for half in range(HALVES):
         load_copy(half).start()
-    for copy in small[1:]:
-        copy.start()
-
     lane = lax.broadcasted_iota(jnp.int32, (8, 128), 1)
     lower_half = lane < 64
 
@@ -103,24 +100,25 @@
                     if above[a] < (2, 2, 4)[a]:
                         bits = jnp.where(lower_half, mask_of(a, *above), own)
                     else:
-                        bits = jnp.where(lower_half, 0, own)
+                        bits = jnp.full((8, 128), own, jnp.int32)
                     index_v[a, e] = (lane ^ 64) ^ bits
                     if (i, j, k)[a] == 0:
                         parity = j if a == 2 else k % 2
                         slot = (j * 4 + k, i * 4 + k, i * 2 + j)[a]
                         face_index_v[a, slot] = lane ^ (own ^ (64 * parity))
 
-    for a in range(3):
-        for there, direction in ((has_above[a], 0), (has_below[a], 1)):
-
-            @pl.when(jnp.logical_not(there))
-            def _():
-                for turn in range(ROUNDS):
-                    for half in range(HALVES):
-                        if a < 2:
-                            got_xy[turn, half, 2 * a + direction] = jnp.zeros(got_xy.shape[3:], jnp.float32)
-                        else:
-                            got_z[turn, half, direction] = jnp.zeros(got_z.shape[3:], jnp.float32)
+    def clear(turns):
+        for a in range(3):
+            for there, direction in ((has_above[a], 0), (has_below[a], 1)):
+
+                @pl.when(jnp.logical_not(there))
+                def _():
+                    for turn in turns:
+                        for half in range(HALVES):
+                            if a < 2:
+                                got_xy[turn, half, 2 * a + direction] = jnp.zeros(got_xy.shape[3:], jnp.float32)
+                            else:
+                                got_z[turn, half, direction] = jnp.zeros(got_z.shape[3:], jnp.float32)
 
     def face_copy(turn, half, a, direction):
         channel = 2 * a + direction
@@ -129,7 +127,7 @@
         else:
             source, target = sent_z.at[turn, half, direction], got_z.at[turn, half, direction]
         return pltpu.make_async_remote_copy(
-            source, target, send_sem.at[turn, half, channel], recv_sem.at[turn, half, channel],
+            source, target, send_sem.at[half, channel], recv_sem.at[turn % 2, half, channel],
             device_id={AXES[a]: position[a] + (1 if direction else -1)}, device_id_type=pl.DeviceIdType.MESH,
         )
 
@@ -138,8 +136,15 @@
 
     def gathered(value, index):
         index = jnp.broadcast_to(index, value.shape)
-        return jnp.take_along_axis(
-            value.reshape(-1, 128), index.reshape(-1, 128), axis=1, mode="promise_in_bounds"
+        return lax.gather(
+            value.reshape(-1, 128),
+            index.reshape(-1, 128, 1),
+            lax.GatherDimensionNumbers(
+                offset_dims=(), collapsed_slice_dims=(1,), start_index_map=(1,),
+                operand_batching_dims=(0,), start_indices_batching_dims=(0,),
+            ),
+            slice_sizes=(1, 1),
+            mode=lax.GatherScatterMode.PROMISE_IN_BOUNDS,
         ).reshape(value.shape)
 
     def edge(value, a, last):
@@ -152,12 +157,17 @@
     def shaped(value):
         return value.reshape((2, 2, 4) + value.shape[1:])
 
+    def face_index(a, parity):
+        lead = (2,) if a == 2 else (2, 2)
+        index = face_index_v[a, : 4 if a == 2 else 8].reshape(lead + (2, 8, 128))
+        return lax.index_in_dim(index, parity, len(lead), keepdims=True)
+
     def pack(turn, half, source, a):
-        swapped = gathered(source, index_v[a][:, None])
-        swapped_v[half, a] = swapped
-        first, second = edge(shaped(swapped), a, False)
-        down = jnp.where(lower_half, rolled(first), second)
-        up = jnp.where(lower_half, edge(shaped(swapped), a, True)[0], edge(shaped(source), a, True)[1])
+        source = shaped(source)
+        first, second = edge(source, a, False)
+        down = jnp.where(lower_half, gathered(first, face_index(a, 0)), gathered(second, face_index(a, 1)))
+        first, second = edge(source, a, True)
+        up = jnp.where(lower_half, rolled(first), second)
         if a < 2:
             sent_xy[turn, half, 2 * a] = down.reshape(sent_xy.shape[3:])
             sent_xy[turn, half, 2 * a + 1] = up.reshape(sent_xy.shape[3:])
@@ -165,6 +175,19 @@
             sent_z[turn, half, 0] = down.reshape(sent_z.shape[3:])
             sent_z[turn, half, 1] = up.reshape(sent_z.shape[3:])
 
+    def prepare(half, source_of, base_ref, sign):
+        for a in range(3):
+            source = source_of(a)
+            swapped = shaped(gathered(source, index_v[a][:, None]))
+            count = swapped.shape[a]
+            zero = jnp.zeros_like(lax.slice_in_dim(swapped, 0, 1, axis=a))
+            from_below = jnp.concatenate([zero, lax.slice_in_dim(swapped, 0, count - 1, axis=a)], a)
+            from_above = jnp.concatenate([lax.slice_in_dim(swapped, 1, count, axis=a), zero], a)
+            total = source + jnp.where(lower_half, from_below, from_above).reshape(source.shape)
+            if base_ref is not None:
+                total = base_ref[half, a] + sign * total
+            local_v[half, a] = total
+
     def send(turn, half, a):
         for there, direction in ((has_below[a], 0), (has_above[a], 1)):
 
@@ -172,57 +195,61 @@
             def _():
                 face_copy(turn, half, a, direction).start()
 
+    def sent(turn, half):
+        for a in ORDER:
+            for there, direction in ((has_below[a], 0), (has_above[a], 1)):
+
+                @pl.when(there)
+                def _():
+                    face_copy(turn, half, a, direction).wait_send()
+
     def receive(turn, half):
-        for a in range(3):
-
-            @pl.when(has_below[a])
-            def _():
-                face_copy(turn, half, a, 0).wait_send()
-                face_copy(turn, half, a, 1).wait_recv()
-
-            @pl.when(has_above[a])
-            def _():
-                face_copy(turn, half, a, 1).wait_send()
-                face_copy(turn, half, a, 0).wait_recv()
-
-    def assembled_sum(turn, half, source, a):
-        swapped = shaped(swapped_v[half, a])
+        for a in ORDER:
+            for there, direction in ((has_below[a], 1), (has_above[a], 0)):
+
+                @pl.when(there)
+                def _():
+                    face_copy(turn, half, a, direction).wait_recv()
+
+    def assembled_sum(turn, half, a, sign=1):
+        local = shaped(local_v[half, a])
         if a < 2:
             down, up = got_xy[turn, half, 2 * a], got_xy[turn, half, 2 * a + 1]
             lead = (2, 2)
         else:
             down, up = got_z[turn, half, 0], got_z[turn, half, 1]
             lead = (2,)
-        face_index = face_index_v[a, : 4 if a == 2 else 8].reshape(lead + (2, 8, 128))
         wide = lead + down.shape[1:]
         down, up = down.reshape(wide), up.reshape(wide)
         top = jnp.stack([rolled(down), down], len(lead))
-        low = jnp.stack(
-            [gathered(up, lax.index_in_dim(face_index, parity, len(lead), keepdims=True)) for parity in range(2)],
-            len(lead),
-        )
-        layer = list(swapped.shape)
+        low = jnp.stack([gathered(up, face_index(a, parity)) for parity in range(2)], len(lead))
+        layer = list(local.shape)
         layer[a] = 1
-        top, low = top.reshape(layer), low.reshape(layer)
-        count = swapped.shape[a]
-        from_below = jnp.concatenate([low, lax.slice_in_dim(swapped, 0, count - 1, axis=a)], a)
-        from_above = jnp.concatenate([lax.slice_in_dim(swapped, 1, count, axis=a), top], a)
-        return source + jnp.where(lower_half, from_below, from_above).reshape(source.shape)
+        low = jnp.where(lower_half, low, 0.0).reshape(layer)
+        top = jnp.where(lower_half, 0.0, top).reshape(layer)
+        count = local.shape[a]
+        pieces = [
+            lax.slice_in_dim(local, 0, 1, axis=a) + sign * low,
+            lax.slice_in_dim(local, count - 1, count, axis=a) + sign * top,
+        ]
+        if count > 2:
+            pieces.insert(1, lax.slice_in_dim(local, 1, count - 1, axis=a))
+        return jnp.concatenate(pieces, a).reshape((16,) + local.shape[3:])
 
     def columns(a):
         return slice(a * 128, (a + 1) * 128)
 
     def multiply_and_send(turn, half, row_parts, matrix_ref, factor_ref):
         rows = jnp.concatenate([part for parts in row_parts for part in parts], -1)
-        for group in GROUPS:
-            for a in group:
-                out = jnp.dot(rows, matrix_ref[a], preferred_element_type=jnp.float32)
-                out = out[:, :128] + out[:, 128:]
-                piece = out.reshape(16, groups, 8, 128) * factor_ref[:, :, columns(a)][:, None]
-                y_v[half, a] = piece
-                pack(turn, half, piece, a)
-            for a in group:
-                send(turn, half, a)
+        for a in ORDER:
+            blocks = [rows] if a != ORDER[-1] else [rows[: rows.shape[0] // 2], rows[rows.shape[0] // 2 :]]
+            outs = [jnp.dot(block, matrix_ref[a], preferred_element_type=jnp.float32) for block in blocks]
+            out = jnp.concatenate([out[:, :128] + out[:, 128:] for out in outs], 0)
+            piece = out.reshape(16, groups, 8, 128) * factor_ref[:, :, columns(a)][:, None]
+            y_v[half, a] = piece
+            pack(turn, half, piece, a)
+        for a in ORDER:
+            send(turn, half, a)
 
     def set_matrix(value, matrix_ref):
         high, low = parts_of(value)
@@ -241,11 +268,15 @@
 
     for half in range(HALVES):
         load_copy(half).wait()
-        for a in range(3):
+        if half == 0:
+            for copy in small[1:]:
+                copy.start()
+        for a in ORDER:
             pack(0, half, half_rows(load_v, half, a), a)
-        for a in range(3):
+        for a in ORDER:
             send(0, half, a)
 
+    clear(range(1))
     small[1].wait()
     small[2].wait()
     for i in range(2):
@@ -273,39 +304,59 @@
         prolong_four_ref[...].T, small_dot(coarse_four_ref[...], prolong_four_ref[...])
     ) + small_dot(prolong_two_ref[...].T, small_dot(coarse_two_ref[...], prolong_two_ref[...]))
     set_matrix(fine_weight * matrix_v[0] + coarse_weight * coarse, smoother_v)
-    small[8].wait()
-    set_matrix(matrix_v[1], operator_v)
 
     def flat_parts(value):
         return parts_of(value.reshape(-1, 128))
 
+    def made(half):
+        return lambda a: y_v[half, a]
+
+    for half in range(HALVES):
+        prepare(half, lambda a, half=half: half_rows(load_v, half, a), None, 1)
+    for half in range(HALVES):
+        sent(0, half)
     for half in range(HALVES):
         receive(0, half)
         row_parts = []
         for a in range(3):
-            total = assembled_sum(0, half, half_rows(load_v, half, a), a)
+            total = assembled_sum(0, half, a)
             assembled_v[half, a] = total
             row_parts.append(flat_parts(total * keep_inverse_v[:, :, columns(a)][:, None]))
         multiply_and_send(1, half, row_parts, smoother_v, inverse_v)
+    clear(range(1, ROUNDS))
+    small[8].wait()
+    set_matrix(matrix_v[1], operator_v)
+    for half in range(HALVES):
+        prepare(half, made(half), None, 1)
+    for half in range(HALVES):
+        sent(1, half)
     for half in range(HALVES):
         receive(1, half)
         row_parts = []
         for a in range(3):
-            total = assembled_sum(1, half, y_v[half, a], a)
+            total = assembled_sum(1, half, a)
             first_v[half, a] = total
             row_parts.append(flat_parts(total * keep_scale_v[:, :, columns(a)][:, None]))
         multiply_and_send(2, half, row_parts, operator_v, scale_v)
     for half in range(HALVES):
+        prepare(half, made(half), assembled_v, -1)
+    for half in range(HALVES):
+        sent(2, half)
+    for half in range(HALVES):
         receive(2, half)
         row_parts = []
         for a in range(3):
-            total = assembled_v[half, a] - assembled_sum(2, half, y_v[half, a], a)
+            total = assembled_sum(2, half, a, -1)
             row_parts.append(flat_parts(total * keep_inverse_v[:, :, columns(a)][:, None]))
         multiply_and_send(3, half, row_parts, smoother_v, inverse_v)
     for half in range(HALVES):
+        prepare(half, made(half), first_v, 1)
+    for half in range(HALVES):
+        sent(3, half)
+    for half in range(HALVES):
         receive(3, half)
         for a in range(3):
-            total = first_v[half, a] + assembled_sum(3, half, y_v[half, a], a)
+            total = assembled_sum(3, half, a)
             out_ref[:, half * groups : (half + 1) * groups, :, columns(a)] = total * keep_v[:, :, columns(a)][:, None]
 
 
@@ -346,8 +397,8 @@
             pltpu.VMEM((ROUNDS, HALVES, 2, 2, local, 8, 128), f32),
             pltpu.SemaphoreType.DMA((HALVES,)),
             pltpu.SemaphoreType.DMA((9,)),
-            pltpu.SemaphoreType.DMA((ROUNDS, HALVES, 6)),
-            pltpu.SemaphoreType.DMA((ROUNDS, HALVES, 6)),
+            pltpu.SemaphoreType.DMA((HALVES, 6)),
+            pltpu.SemaphoreType.DMA((2, HALVES, 6)),
         ],
         compiler_params=pltpu.CompilerParams(collective_id=0, has_side_effects=True, vmem_limit_bytes=32 * 1024 * 1024),
     )(*(pltpu.with_memory_space_constraint(value, pltpu.HBM) for value in (

time: 25.8 us -> 24.7 us (0.957)
  Pallas kernels: 24.8 us -> 23.7 us
    pallas_call x1, Pallas kernels: 24.8 us -> 23.7 us  [body(): pl.pallas_call(kernel, out_shape=pltpu.VMEM((elements, groups, 8, nodes),...]
where the time goes in v3:
time: 24.7 us; the launch traced here: 24.6 us
  Pallas kernels  23.7 us (96%)
  local copies, waits for them, and re-layouts  0.88 us (4%)
    pallas_call x1, Pallas kernels, body(): pl.pallas_call(kernel, out_shape=pltpu.VMEM((elements, groups, 8, nodes),...  23.7 us
    unnamed x1, local copies, waits for them, and re-layouts  0.88 us

profile of v3, /device:TPU:1, one launch (start us, length us, event | category | flops | bytes accessed | tf_op | source)
XLA Modules:
  0.0 24.6 jit_solution(3221249894392392444)
XLA Ops:
  0.0 23.7 %shard_map.100 = f32[16,4,8,384]{3,2,1,0:T(8,128)S(1)} custom-call(f32[16,4,8,384]{3,2,1,0:T(8,128)} %bitcast.6, f32[384,384]{1,0:T(8,128)} %fine_matrix_hbm.1, f32[384,384]{1,0:T(8,128)} %fine_inverse_hbm.1, f32[2,2,4,384]{3,2,1,0:T(4,128)} %scaling_hbm.1, f32[98,384]{1,0:T(8,128)} %bitcast.7, f32[98,98]{1,0:T(8,128)} %coarse_four_hbm.1, ...), custom_call_target="tpu_custom_call" | custom-call | tf_op jit(solution)/shard_map/pallas_call | solution.py:373
  23.7 0.9 %copy.12 = f32[2,2,4,32,384]{4,3,2,1,0:T(8,128)} copy(f32[2,2,4,32,384]{4,3,2,1,0:T(8,128)S(1)} %bitcast.5) | data formatting | bytes 1572864
